TPU v7x, 32 devices: a whole 2x2x4 slice. The times are simulated.
32 devices in a mesh: gx: 4 (over y, core), yz: 8 (over z, x).
Axes of the slice: x: 2, y: 2, z: 4, core: 2. Of those that a mesh axis runs over, the one named last changes fastest.
Arguments:
- composition: float32 [4096, 20, 128], P(('gx', 'yz')), may hold values from -6 to 6
- particle_mass: float32 [4096, 128], P(('gx', 'yz')), may hold values from 0.5 to 2
- mixing_rate: float32 [4096, 128], P(('gx', 'yz')), may hold values from 0.2 to 3
- cell_index: int32 [4096, 128], P(('gx', 'yz')), may hold values from 0 to 4095, as said below
- section_counts: int32 [4096], P(('gx', 'yz')), may hold values from 1 to 6, as said below
- block_shuffle: int32 [32, 128], P(('gx', 'yz')), may hold values from 0 to 127, as said below
- batch_inverse: float32 [32, 20, 20], P(('gx', 'yz')), may hold values from -1.25 to 1.25
- rate_exponents: float32 [84, 20], replicated, may hold values from -1.25 to 1.25
- stoichiometry: float32 [20, 84], replicated, may hold values from -0.625 to 0.625
Outputs:
- reacted: float32 [4096, 20, 128], P(('gx', 'yz'))
Inputs may be any that keep to these rules, and one draw needn't show every extreme that they name: `cell_index`: A particle of the device at index i of gx and j of yz (d = i * 8 + j) lies in slab i - 1, i or i + 1, slab s holding cells s * 128 * 8 to (s + 1) * 128 * 8 - 1; that device's first 128 particles lie one each in cells d * 128 to d * 128 + 127. `section_counts`: some block has exactly 6 sections. `block_shuffle`: each row is a permutation of 0 to 127.
All inputs are finite; a program needn't handle non-finite values.
Results may differ from a plain program's by a relative error of at most 0.0011.
Values sent between devices are 32-bit elements; how exact they have to be, the bound alone decides.
No kernel may reach another device: no remote copies, remote signals or barrier semaphores. Data moves between devices by JAX's collectives and lax.ppermute only.
A program may use at most 128 MiB of HBM per device.

v0:
```python
import jax
import jax.numpy as jnp
from jax import lax
from jax.sharding import PartitionSpec as P

CELL_DEV = 128
step_size = 0.25


def extended_2(cells, sides, width):
    for axis, dim in sides:
        count = lax.axis_size(axis)
        ends = count - 1
        head = lax.slice_in_dim(cells, 0, width, axis=dim)
        tail = lax.slice_in_dim(cells, cells.shape[dim] - width, cells.shape[dim], axis=dim)
        cells = jnp.concatenate(
            [
                lax.ppermute(tail, axis, [(i, (i + 1) % count) for i in range(ends)]),
                cells,
                lax.ppermute(head, axis, [((i + 1) % count, i) for i in range(ends)]),
            ],
            axis=dim,
        )
    return cells


def section_update(current, matrices, rate_exponents, stoichiometry):
    progress = jnp.tanh(
        jnp.einsum("rj,bjk->brk", rate_exponents, current, precision=lax.Precision.HIGHEST)
    )
    forcing = jnp.einsum("ir,brk->bik", stoichiometry, progress, precision=lax.Precision.HIGHEST)
    return jnp.einsum("bij,bjk->bik", matrices, forcing, precision=lax.Precision.HIGHEST)


def advance_blocks(current, counts, matrices, rate_exponents, stoichiometry):
    ordering = jnp.argsort(-counts, stable=True)
    restore = jnp.argsort(ordering, stable=True)
    current = current[ordering]
    counts = counts[ordering]
    matrices = matrices[ordering]
    batch_width = min(current.shape[0], 64)

    def one_section(section_index, current):
        active = jnp.sum((counts > section_index).astype(jnp.int32))
        batches = (active + batch_width - 1) // batch_width

        def one_batch(number, current):
            offset = number * batch_width
            chosen = lax.dynamic_slice_in_dim(current, offset, batch_width, 0)
            chosen_matrices = lax.dynamic_slice_in_dim(matrices, offset, batch_width, 0)
            chosen_counts = lax.dynamic_slice_in_dim(counts, offset, batch_width, 0)
            updated = chosen + step_size * section_update(
                chosen, chosen_matrices, rate_exponents, stoichiometry
            )
            chosen = jnp.where((chosen_counts > section_index)[:, None, None], updated, chosen)
            return lax.dynamic_update_slice_in_dim(current, chosen, offset, 0)

        return lax.fori_loop(0, batches, one_batch, current)

    current = lax.fori_loop(0, jnp.max(counts), one_section, current)
    return current[restore]


def split_three(values):
    upper = values.astype(jnp.bfloat16)
    rest = values - upper.astype(jnp.float32)
    middle = rest.astype(jnp.bfloat16)
    lower = (rest - middle.astype(jnp.float32)).astype(jnp.bfloat16)
    return jnp.stack([upper, middle, lower], axis=0)


def local(
    composition,
    particle_mass,
    mixing_rate,
    cell_index,
    section_counts,
    block_shuffle,
    batch_inverse,
    rate_exponents,
    stoichiometry,
):
    block_total, species, lane_count = composition.shape
    columns = lax.axis_size("yz")
    slab_cells = CELL_DEV * columns
    first_cell = (lax.axis_index("gx") - 1) * slab_cells
    local_cell = cell_index - first_cell
    moments = species + 1
    low_width = min(256, slab_cells)
    high_count = 3 * slab_cells // low_width
    particles = block_total * lane_count
    tile = min(1024, particles)
    turns = particles // tile
    tile_blocks = tile // lane_count
    high_part = (local_cell // low_width).reshape(turns, tile)
    low_part = (local_cell % low_width).reshape(turns, tile)
    high_iota = jnp.arange(high_count, dtype=jnp.int32)
    low_iota = jnp.arange(low_width, dtype=jnp.int32)
    weighted = composition * particle_mass[:, None, :]
    values = jnp.concatenate([particle_mass[:, None, :], weighted], axis=1)
    values = (
        values.reshape(turns, tile_blocks, moments, lane_count)
        .transpose(0, 2, 1, 3)
        .reshape(turns, moments, tile)
    )

    def add_tile(number, total):
        pieces = split_three(values[number]).reshape(3 * moments, tile)
        high_table = (high_part[number][None, :] == high_iota[:, None]).astype(jnp.bfloat16)
        low_table = (low_part[number][:, None] == low_iota[None, :]).astype(jnp.bfloat16)
        spread = (pieces[:, None, :] * high_table[None, :, :]).reshape(
            3 * moments * high_count, tile
        )
        return total + jnp.dot(spread, low_table, preferred_element_type=jnp.float32)

    summed = lax.fori_loop(
        0, turns, add_tile, jnp.zeros((3 * moments * high_count, low_width), jnp.float32)
    )
    summed = summed.reshape(3, moments, 3 * slab_cells)
    partial_value = (
        (summed[0] + summed[1] + summed[2]).reshape(moments, 3, slab_cells).transpose(1, 0, 2)
    )
    extended = extended_2(partial_value, (("gx", 0),), 1)
    totals = lax.psum_scatter(
        extended[2] + extended[0] + extended[4], "yz", scatter_dimension=1, tiled=True
    )
    cell_means = totals[1:] / totals[0][None, :]
    gathered = lax.all_gather(cell_means[None], "yz", axis=2, tiled=True)
    nearby = extended_2(gathered, (("gx", 0),), 1)
    means_flat = jnp.moveaxis(nearby, 0, 1).reshape(species, 3 * slab_cells)
    mean_parts = split_three(means_flat).reshape(3, species * high_count, low_width)

    def look_tile(inputs):
        high_row, low_row = inputs
        low_table = (low_iota[:, None] == low_row[None, :]).astype(jnp.bfloat16)
        picked = jnp.dot(mean_parts[0], low_table, preferred_element_type=jnp.float32)
        picked = picked + jnp.dot(mean_parts[1], low_table, preferred_element_type=jnp.float32)
        picked = picked + jnp.dot(mean_parts[2], low_table, preferred_element_type=jnp.float32)
        high_table = (high_row[None, :] == high_iota[:, None]).astype(jnp.float32)
        return jnp.sum(picked.reshape(species, high_count, tile) * high_table[None], axis=1)

    looked = lax.map(look_tile, (high_part, low_part))
    looked = (
        looked.reshape(turns, species, tile_blocks, lane_count)
        .transpose(0, 2, 1, 3)
        .reshape(block_total, species, lane_count)
    )
    mixed_state = looked + (composition - looked) * jnp.exp(-mixing_rate)[:, None, :]
    ordering = block_shuffle[0]
    outgoing = mixed_state[ordering]
    outgoing_counts = section_counts[ordering].astype(jnp.float32)
    arrived, arrived_counts = (
        lax.all_to_all(outgoing, ("gx", "yz"), split_axis=0, concat_axis=0, tiled=True),
        lax.all_to_all(outgoing_counts, ("gx", "yz"), split_axis=0, concat_axis=0, tiled=True),
    )
    matrices = jnp.broadcast_to(batch_inverse[0], (block_total, species, species))
    reacted = advance_blocks(
        arrived, arrived_counts.astype(jnp.int32), matrices, rate_exponents, stoichiometry
    )
    returned = lax.all_to_all(reacted, ("gx", "yz"), split_axis=0, concat_axis=0, tiled=True)
    return returned[jnp.argsort(ordering, stable=True)]


def solution(mesh):
    in_specs = (
        P(("gx", "yz"), None, None),
        P(("gx", "yz"), None),
        P(("gx", "yz"), None),
        P(("gx", "yz"), None),
        P(("gx", "yz")),
        P(("gx", "yz"), None),
        P(("gx", "yz"), None, None),
        P(),
        P(),
    )
    out_specs = P(("gx", "yz"), None, None)
    return jax.shard_map(local, mesh=mesh, in_specs=in_specs, out_specs=out_specs, check_vma=False)
```

profile of v0, /device:TPU:0, one launch (start us, length us, event | category | flops | bytes accessed | tf_op | source)
XLA Modules:
  0.0 422.8 jit_solution(2543802282157748160)
XLA Ops:
  10.6 83.8 %while.68 = (s32[]{:T(128)}, f32[756,256]{1,0:T(8,128)S(1)}, f32[16,21,1024]{2,0,1:T(8,128)S(1)}, s32[16,1024]{1,0:T(8,128)}, s32[16,1024]{1,0:T(8,128)}, /*index=5*/s32[]{:T(128)}, s32[]{:T(128)}) while((s32[]{:T(128)}, f32[756,256]{1,0:T(8,128)S(1)}, f32[16,21,1024]{2,0,1:T(8,128)S(1)}, s32[16,1024]{1,0:T(8,128)}, ...), condition=%wide.region_1.2_spmd.clone, body=%wide.region_0.1_spmd.clone.sunk | while | flops 398089216 | bytes 19943576 | solution.py:116
  11.9 1.5 mul.117
  13.4 2.4 convolution_add_fusion.6
  17.1 1.5 mul.117
  18.6 2.4 convolution_add_fusion.6
  22.3 1.5 mul.117
  23.8 2.4 convolution_add_fusion.6
  27.6 1.5 mul.117
  29.1 2.4 convolution_add_fusion.6
  34.3 2.4 convolution_add_fusion.6
  39.5 2.4 convolution_add_fusion.6
  44.8 2.4 convolution_add_fusion.6
  50.0 2.4 convolution_add_fusion.6
  55.3 2.4 convolution_add_fusion.6
  60.5 2.4 convolution_add_fusion.6
  65.7 2.4 convolution_add_fusion.6
  71.0 2.4 convolution_add_fusion.6
  76.2 2.4 convolution_add_fusion.6
  81.4 2.4 convolution_add_fusion.6
  86.7 2.4 convolution_add_fusion.6
  91.9 2.4 convolution_add_fusion.6
  94.7 2.4 collective-permute-start
  98.4 4.0 collective-permute-done.1
  105.3 7.6 %all-to-all-start.1 = ((f32[32,4,1]{1,2,0:T(1,128)}), f32[32,4,1]{1,2,0:T(1,128)S(1)}, u32[]{:S(2)}, u32[]{:S(2)}) async-start(f32[32,4,1]{1,2,0:T(1,128)} %bitcast.15), calls=%async_computation.2 | async-start | bytes 32768 | tf_op jit(solution)/shard_map/all_to_all | solution.py:154
  113.0 52.3 %reduce-scatter.2.cloned.1.call-done = f32[21,128]{1,0:T(8,128)} async-done(((f32[21,1024]{1,0:T(8,128)}), f32[21,128]{1,0:T(8,128)}) %reduce-scatter.2.cloned.1.call-update) | async-done | bytes 10768 | tf_op jit(solution)/shard_map/reduce_scatter | solution.py:124
  166.7 30.5 %all-gather = f32[20,1024]{1,0:T(8,128)S(1)} all-gather(f32[20,128]{1,0:T(8,128)S(1)} %slice_divide_fusion), channel_id=2, replica_groups=mesh['gx'=4,'yz'=8] {'yz'}, dimensions={1}, use_global_device_ids=true | all-gather | bytes 92160 | tf_op jit(solution)/shard_map/all_gather | solution.py:128
  199.8 3.6 collective-permute-done.3
  203.9 47.6 %while.67 = (s32[]{:T(128)}, f32[16,20,1024]{2,1,0:T(8,128)}, s32[16,1024]{1,0:T(8,128)}, bf16[3,240,256]{2,1,0:T(8,128)(2,1)S(1)}, s32[16,1024]{1,0:T(8,128)}, /*index=5*/s32[]{:T(128)}) while((s32[]{:T(128)}, f32[16,20,1024]{2,1,0:T(8,128)}, s32[16,1024]{1,0:T(8,128)}, bf16[3,240,256]{2,1,0:T(8,128)(2,1)S(1)}, ...), condition=%wide.region_5.6_spmd.clone, body=%wide.region_3.5_spmd.clone.sunk | while | flops 379260928 | bytes 8626761 | solution.py:142
  251.5 1.5 reshape.285
  255.2 1.9 gather_fusion
  257.1 5.7 %all-to-all-start = ((f32[128,20,128]{2,1,0:T(8,128)}), f32[128,20,128]{2,1,0:T(8,128)}, u32[]{:S(2)}, u32[]{:S(2)}) async-start(f32[128,20,128]{2,1,0:T(8,128)} %gather_fusion), calls=%async_computation.1 | async-start | bytes 3145728 | tf_op jit(solution)/shard_map/all_to_all | solution.py:153
  263.0 2.5 sort.45
  267.7 2.5 sort.46
  270.8 30.7 %all-to-all-done = f32[128,20,128]{2,1,0:T(8,128)} async-done(((f32[128,20,128]{2,1,0:T(8,128)}), f32[128,20,128]{2,1,0:T(8,128)}, u32[]{:S(2)}, u32[]{:S(2)}) %all-to-all-start) | async-done | bytes 1310752 | tf_op jit(solution)/shard_map/all_to_all | solution.py:153
  301.5 2.1 gather_fusion.2
  303.6 66.9 %while.66 = (s32[]{:T(128)}, f32[128,20,128]{2,1,0:T(8,128)S(1)}, s32[]{:T(128)}, s32[128]{0:T(128)S(1)}, f32[128,20,20]{2,1,0:T(8,128)S(1)}, /*index=5*/f32[84,...) while((s32[]{:T(128)}, f32[128,20,128]{2,1,0:T(8,128)S(1)}, ...), condition=%wide.region_12.13_spmd, body=%wide.region_8.12_spmd.sunk | while | flops 370115008 | bytes 10114534 | solution.py:60
  305.7 12.1 %while.69 = (s32[]{:T(128)}, f32[128,20,128]{2,1,0:T(8,128)S(1)}, s32[]{:T(128)}, s32[128]{0:T(128)S(1)}, s32[]{:T(128)}, /*index=5*/f32[128,20,20]{2,1,0:T(8,12...) while((s32[]{:T(128)}, f32[128,20,128]{2,1,0:T(8,128)S(1)}, ...), condition=%wide.region_11.11_spmd, body=%wide.region_10.10_spmd.sunk | while | flops 370114624 | bytes 10113583 | solution.py:58
  305.8 2.4 fusion.82
  308.2 2.1 fusion.83
  311.8 2.4 fusion.82
  314.2 2.1 fusion.83
  319.8 12.0 %while.69 = (s32[]{:T(128)}, f32[128,20,128]{2,1,0:T(8,128)S(1)}, s32[]{:T(128)}, s32[128]{0:T(128)S(1)}, s32[]{:T(128)}, /*index=5*/f32[128,20,20]{2,1,0:T(8,12...) while((s32[]{:T(128)}, f32[128,20,128]{2,1,0:T(8,128)S(1)}, ...), condition=%wide.region_11.11_spmd, body=%wide.region_10.10_spmd.sunk | while | flops 370114624 | bytes 10113583 | solution.py:58
  319.8 2.4 fusion.82
  322.2 2.1 fusion.83
  325.8 2.4 fusion.82
  328.3 2.1 fusion.83
  333.8 12.0 %while.69 = (s32[]{:T(128)}, f32[128,20,128]{2,1,0:T(8,128)S(1)}, s32[]{:T(128)}, s32[128]{0:T(128)S(1)}, s32[]{:T(128)}, /*index=5*/f32[128,20,20]{2,1,0:T(8,12...) while((s32[]{:T(128)}, f32[128,20,128]{2,1,0:T(8,128)S(1)}, ...), condition=%wide.region_11.11_spmd, body=%wide.region_10.10_spmd.sunk | while | flops 370114624 | bytes 10113583 | solution.py:58
  333.8 2.4 fusion.82
  336.3 2.1 fusion.83
  339.9 2.4 fusion.82
  342.3 2.1 fusion.83
  347.9 6.0 %while.69 = (s32[]{:T(128)}, f32[128,20,128]{2,1,0:T(8,128)S(1)}, s32[]{:T(128)}, s32[128]{0:T(128)S(1)}, s32[]{:T(128)}, /*index=5*/f32[128,20,20]{2,1,0:T(8,12...) while((s32[]{:T(128)}, f32[128,20,128]{2,1,0:T(8,128)S(1)}, ...), condition=%wide.region_11.11_spmd, body=%wide.region_10.10_spmd.sunk | while | flops 370114624 | bytes 10113583 | solution.py:58
  347.9 2.4 fusion.82
  350.3 2.1 fusion.83
  355.9 6.0 %while.69 = (s32[]{:T(128)}, f32[128,20,128]{2,1,0:T(8,128)S(1)}, s32[]{:T(128)}, s32[128]{0:T(128)S(1)}, s32[]{:T(128)}, /*index=5*/f32[128,20,20]{2,1,0:T(8,12...) while((s32[]{:T(128)}, f32[128,20,128]{2,1,0:T(8,128)S(1)}, ...), condition=%wide.region_11.11_spmd, body=%wide.region_10.10_spmd.sunk | while | flops 370114624 | bytes 10113583 | solution.py:58
  355.9 2.4 fusion.82
  358.4 2.1 fusion.83
  363.9 6.0 %while.69 = (s32[]{:T(128)}, f32[128,20,128]{2,1,0:T(8,128)S(1)}, s32[]{:T(128)}, s32[128]{0:T(128)S(1)}, s32[]{:T(128)}, /*index=5*/f32[128,20,20]{2,1,0:T(8,12...) while((s32[]{:T(128)}, f32[128,20,128]{2,1,0:T(8,128)S(1)}, ...), condition=%wide.region_11.11_spmd, body=%wide.region_10.10_spmd.sunk | while | flops 370114624 | bytes 10113583 | solution.py:58
  363.9 2.4 fusion.82
  366.4 2.1 fusion.83
  370.5 1.9 gather_fusion.5
  372.5 2.7 all-to-all-start.2
  375.2 2.5 sort.47
  377.7 36.1 %all-to-all-done.2 = f32[128,20,128]{2,1,0:T(8,128)S(1)} async-done(((f32[128,20,128]{2,1,0:T(8,128)}), f32[128,20,128]{2,1,0:T(8,128)S(1)}, u32[]{:S(2)}, u32[]{:S(2)}) %all-to-all-start.2) | async-done | bytes 1310752 | tf_op jit(solution)/shard_map/all_to_all | solution.py:160
  (427 shorter events, 122.0 us)
Async XLA Ops:
  6.5 96.8 %copy-start = (s32[128]{0:T(128)S(1)}, s32[128]{0:T(128)}, u32[]{:S(2)}) copy-start(s32[128]{0:T(128)} %param.21) | copy-start | bytes 1540
  6.5 158.7 %reduce-scatter.2.cloned.1.call-start = ((), (), s32[]{:S(2)}) async-start(), calls=%async_computation.4 | async-start | bytes 110592 | tf_op jit(solution)/shard_map/reduce_scatter | solution.py:124
  6.5 3.6 copy-start.6
  10.6 1.1 copy-start.4
  13.4 2.4 copy-start.5
  15.8 1.1 copy-start.4
  18.6 2.4 copy-start.5
  21.0 1.1 copy-start.4
  23.8 2.4 copy-start.5
  26.3 1.1 copy-start.4
  29.1 2.4 copy-start.5
  31.5 1.1 copy-start.4
  34.3 2.4 copy-start.5
  36.7 1.1 copy-start.4
  39.5 2.4 copy-start.5
  42.0 1.1 copy-start.4
  44.8 2.4 copy-start.5
  47.2 1.1 copy-start.4
  50.0 2.4 copy-start.5
  52.5 1.1 copy-start.4
  55.2 2.4 copy-start.5
  57.7 1.1 copy-start.4
  60.5 2.4 copy-start.5
  62.9 1.1 copy-start.4
  65.7 2.4 copy-start.5
  68.2 1.1 copy-start.4
  71.0 2.4 copy-start.5
  73.4 1.1 copy-start.4
  76.2 2.4 copy-start.5
  78.6 1.1 copy-start.4
  81.4 2.4 copy-start.5
  83.9 1.1 copy-start.4
  86.7 2.4 copy-start.5
  89.1 1.1 copy-start.4
  91.9 2.4 copy-start.5
  94.4 9.0 %copy-start.9 = (s32[1,128]{1,0:T(1,128)S(1)}, s32[1,128]{1,0:T(1,128)}, u32[]{:S(2)}) copy-start(s32[1,128]{1,0:T(1,128)} %param.22) | copy-start | bytes 1540
  94.4 105.4 %copy-start.7 = (f32[128,128]{1,0:T(8,128)S(1)}, f32[128,128]{1,0:T(8,128)}, u32[]{:S(2)}) copy-start(f32[128,128]{1,0:T(8,128)} %param.19) | copy-start | bytes 196612
  94.7 3.7 collective-permute-start
  97.1 5.3 %collective-permute-start.1 = (f32[1,21,1024]{2,0,1:T(1,128)S(1)}, f32[1,21,1024]{2,0,1:T(1,128)S(1)}, u32[]{:S(2)}, u32[]{:S(2)}) collective-permute-start(f32[1,21,1024]{2,0,1:T(1,128)S(1)} %get-tuple-element.518), channel_id=1, source_target_pairs={{8,0},{16,8},{24,16},{9,1},{17,9},{25,17},{10,2},{18,10},{26,18},{... | collective-permute-start | bytes 258056 | tf_op jit(solution)/shard_map/ppermute | solution.py:20
  105.3 151.8 %all-to-all-start.1 = ((f32[32,4,1]{1,2,0:T(1,128)}), f32[32,4,1]{1,2,0:T(1,128)S(1)}, u32[]{:S(2)}, u32[]{:S(2)}) async-start(f32[32,4,1]{1,2,0:T(1,128)} %bitcast.15), calls=%async_computation.2 | async-start | bytes 32768 | tf_op jit(solution)/shard_map/all_to_all | solution.py:154
  197.2 2.6 collective-permute-start.2
  198.5 4.9 %collective-permute-start.3 = (f32[1,20,1024]{2,1,0:T(8,128)S(1)}, f32[1,20,1024]{2,1,0:T(8,128)S(1)}, u32[]{:S(2)}, u32[]{:S(2)}) collective-permute-start(f32[1,20,1024]{2,1,0:T(8,128)S(1)} %bitcast.102), channel_id=1, source_target_pairs={{8,0},{16,8},{24,16},{9,1},{17,9},{25,17},{10,2},{18,10},{26,18},{... | collective-permute-start | bytes 245768 | tf_op jit(solution)/shard_map/ppermute | solution.py:20
  253.0 1.3 copy-start.3
  257.1 5.7 %copy-start.8 = (f32[1,20,20]{2,0,1:T(1,128)S(1)}, f32[1,20,20]{2,0,1:T(1,128)}, u32[]{:S(2)}) copy-start(f32[1,20,20]{2,0,1:T(1,128)} %param.23) | copy-start | bytes 4804
  257.1 44.4 %all-to-all-start = ((f32[128,20,128]{2,1,0:T(8,128)}), f32[128,20,128]{2,1,0:T(8,128)}, u32[]{:S(2)}, u32[]{:S(2)}) async-start(f32[128,20,128]{2,1,0:T(8,128)} %gather_fusion), calls=%async_computation.1 | async-start | bytes 3145728 | tf_op jit(solution)/shard_map/all_to_all | solution.py:153
  270.8 32.8 %copy-start.1 = (f32[84,20]{0,1:T(8,128)S(1)}, f32[84,20]{0,1:T(8,128)}, u32[]{:S(2)}) copy-start(f32[84,20]{0,1:T(8,128)} %param.24) | copy-start | bytes 20164
  270.8 32.8 %copy-start.2 = (f32[20,84]{1,0:T(8,128)S(1)}, f32[20,84]{1,0:T(8,128)}, u32[]{:S(2)}) copy-start(f32[20,84]{1,0:T(8,128)} %param.25) | copy-start | bytes 20164
  372.5 41.4 %all-to-all-start.2 = ((f32[128,20,128]{2,1,0:T(8,128)}), f32[128,20,128]{2,1,0:T(8,128)S(1)}, u32[]{:S(2)}, u32[]{:S(2)}) async-start(f32[128,20,128]{2,1,0:T(8,128)} %gather_fusion.5), calls=%async_computation.3 | async-start | bytes 3145728 | tf_op jit(solution)/shard_map/all_to_all | solution.py:160
Sparse Core Ops, SparseCore 0:
  103.4 61.7 reduce-scatter.1
where the time goes:
time: 427 us; the launch traced here: 423 us
  waiting for transfers between devices  127 us (30%)
  matrix products  109 us (26%)
  local copies, waits for them, and re-layouts  83 us (19%)
  blocking collectives  30.5 us (7%)
  other arithmetic  26.1 us (6%)
  starting transfers between devices  22.2 us (5%)
  between operations  13.8 us (3%)
  loops' own time  11.2 us (3%)
    reduce_scatter x1, waiting for transfers between devices, local(): lax.psum_scatter(extended[2] + extended[0] + extended[4], 'yz', scatter_d...  52.3 us
    dot_general x16, matrix products, add_tile(): jnp.dot(spread, low_table, preferred_element_type=jnp.float32)  38.6 us
    all_to_all x1, waiting for transfers between devices, local(): lax.all_to_all(reacted, ('gx', 'yz'), split_axis=0, concat_axis=0, tiled=...  36.1 us
    all_to_all x1, waiting for transfers between devices, local(): lax.all_to_all(outgoing, ('gx', 'yz'), split_axis=0, concat_axis=0, tiled...  30.7 us
    all_gather x1, blocking collectives, local(): gathered = lax.all_gather(cell_means[None], 'yz', axis=2, tiled=True)  30.5 us
    mul x32, local copies, waits for them, and re-layouts, add_tile(): pieces[:, None, :] * high_table[None, :, :]  24.4 us
    dot_general x9, matrix products, section_update(): jnp.einsum('rj,bjk->brk', rate_exponents, current, precision=lax.Precisio...  21.9 us
    dot_general x9, matrix products, section_update(): jnp.einsum('ir,brk->bik', stoichiometry, progress, precision=lax.Precisio...  18.7 us
  transfers between devices with their start and end apart: 8, of which 5 were waited for; matrix products, arithmetic and copies ran while one was open for 16% of the time, Pallas kernels for 0%

commit v1 on v0

--- a/solution.py
+++ b/solution.py
@@ -125,7 +125,9 @@
         extended[2] + extended[0] + extended[4], "yz", scatter_dimension=1, tiled=True
     )
     cell_means = totals[1:] / totals[0][None, :]
-    gathered = lax.all_gather(cell_means[None], "yz", axis=2, tiled=True)
+    block = cell_means[None]
+    tiles = lax.all_gather(block, "yz")
+    gathered = jnp.concatenate(tiles, axis=2)
     nearby = extended_2(gathered, (("gx", 0),), 1)
     means_flat = jnp.moveaxis(nearby, 0, 1).reshape(species, 3 * slab_cells)
     mean_parts = split_three(means_flat).reshape(3, species * high_count, low_width)

time: 427 us -> 427 us (level)
  no operation moved by 1% of the time
where the time goes in v1:
time: 427 us; the launch traced here: 423 us
  waiting for transfers between devices  127 us (30%)
  matrix products  109 us (26%)
  local copies, waits for them, and re-layouts  82.8 us (19%)
  blocking collectives  30.5 us (7%)
  other arithmetic  26.3 us (6%)
  starting transfers between devices  22.1 us (5%)
  between operations  13.8 us (3%)
  loops' own time  11.2 us (3%)
    reduce_scatter x1, waiting for transfers between devices, local(): lax.psum_scatter(extended[2] + extended[0] + extended[4], 'yz', scatter_d...  52.3 us
    dot_general x16, matrix products, add_tile(): jnp.dot(spread, low_table, preferred_element_type=jnp.float32)  38.6 us
    all_to_all x1, waiting for transfers between devices, local(): lax.all_to_all(reacted, ('gx', 'yz'), split_axis=0, concat_axis=0, tiled=...  36.1 us
    all_to_all x1, waiting for transfers between devices, local(): lax.all_to_all(outgoing, ('gx', 'yz'), split_axis=0, concat_axis=0, tiled...  30.7 us
    all_gather x1, blocking collectives, local(): tiles = lax.all_gather(block, 'yz')  30.5 us
    mul x32, local copies, waits for them, and re-layouts, add_tile(): pieces[:, None, :] * high_table[None, :, :]  24.4 us
    dot_general x9, matrix products, section_update(): jnp.einsum('rj,bjk->brk', rate_exponents, current, precision=lax.Precisio...  21.9 us
    dot_general x9, matrix products, section_update(): jnp.einsum('ir,brk->bik', stoichiometry, progress, precision=lax.Precisio...  18.7 us
  transfers between devices with their start and end apart: 8, of which 5 were waited for; matrix products, arithmetic and copies ran while one was open for 16% of the time, Pallas kernels for 0%

profile of v1, /device:TPU:0, one launch (start us, length us, event | category | flops | bytes accessed | tf_op | source)
XLA Modules:
  0.0 422.7 jit_solution(4852000456861776144)
XLA Ops:
  10.6 83.8 %while.68 = (s32[]{:T(128)}, f32[756,256]{1,0:T(8,128)S(1)}, f32[16,21,1024]{2,0,1:T(8,128)S(1)}, s32[16,1024]{1,0:T(8,128)}, s32[16,1024]{1,0:T(8,128)}, /*index=5*/s32[]{:T(128)}, s32[]{:T(128)}) while((s32[]{:T(128)}, f32[756,256]{1,0:T(8,128)S(1)}, f32[16,21,1024]{2,0,1:T(8,128)S(1)}, s32[16,1024]{1,0:T(8,128)}, ...), condition=%wide.region_1.2_spmd.clone, body=%wide.region_0.1_spmd.clone.sunk | while | flops 398089216 | bytes 19943576 | solution.py:116
  11.9 1.5 mul.117
  13.4 2.4 convolution_add_fusion.6
  17.1 1.5 mul.117
  18.6 2.4 convolution_add_fusion.6
  22.3 1.5 mul.117
  23.8 2.4 convolution_add_fusion.6
  27.6 1.5 mul.117
  29.1 2.4 convolution_add_fusion.6
  34.3 2.4 convolution_add_fusion.6
  39.5 2.4 convolution_add_fusion.6
  44.8 2.4 convolution_add_fusion.6
  50.0 2.4 convolution_add_fusion.6
  55.3 2.4 convolution_add_fusion.6
  60.5 2.4 convolution_add_fusion.6
  65.7 2.4 convolution_add_fusion.6
  71.0 2.4 convolution_add_fusion.6
  76.2 2.4 convolution_add_fusion.6
  81.4 2.4 convolution_add_fusion.6
  86.7 2.4 convolution_add_fusion.6
  91.9 2.4 convolution_add_fusion.6
  94.7 2.4 collective-permute-start
  98.4 4.0 collective-permute-done.1
  105.3 7.6 %all-to-all-start.1 = ((f32[32,4,1]{1,2,0:T(1,128)}), f32[32,4,1]{1,2,0:T(1,128)S(1)}, u32[]{:S(2)}, u32[]{:S(2)}) async-start(f32[32,4,1]{1,2,0:T(1,128)} %bitcast.18), calls=%async_computation.2 | async-start | bytes 32768 | tf_op jit(solution)/shard_map/all_to_all | solution.py:156
  113.0 52.3 %reduce-scatter.2.cloned.1.call-done = f32[21,128]{1,0:T(8,128)} async-done(((f32[21,1024]{1,0:T(8,128)}), f32[21,128]{1,0:T(8,128)}) %reduce-scatter.2.cloned.1.call-update) | async-done | bytes 10768 | tf_op jit(solution)/shard_map/reduce_scatter | solution.py:124
  166.7 30.5 %all-gather.1 = f32[8,20,128]{2,1,0:T(8,128)S(1)} all-gather(f32[1,20,128]{2,1,0:T(8,128)S(1)} %fusion.42), channel_id=2, replica_groups=mesh['gx'=4,'yz'=8] {'yz'}, dimensions={0}, use_global_device_ids=true | all-gather | bytes 92160 | tf_op jit(solution)/shard_map/all_gather | solution.py:129
  199.9 3.5 collective-permute-done.3
  203.9 47.6 %while.67 = (s32[]{:T(128)}, f32[16,20,1024]{2,1,0:T(8,128)}, s32[16,1024]{1,0:T(8,128)}, bf16[3,240,256]{2,1,0:T(8,128)(2,1)S(1)}, s32[16,1024]{1,0:T(8,128)}, /*index=5*/s32[]{:T(128)}) while((s32[]{:T(128)}, f32[16,20,1024]{2,1,0:T(8,128)}, s32[16,1024]{1,0:T(8,128)}, bf16[3,240,256]{2,1,0:T(8,128)(2,1)S(1)}, ...), condition=%wide.region_5.6_spmd.clone, body=%wide.region_3.5_spmd.clone.sunk | while | flops 379260928 | bytes 8626761 | solution.py:144
  251.5 1.5 reshape.296
  255.2 1.9 gather_fusion
  257.1 5.5 %all-to-all-start = ((f32[128,20,128]{2,1,0:T(8,128)}), f32[128,20,128]{2,1,0:T(8,128)}, u32[]{:S(2)}, u32[]{:S(2)}) async-start(f32[128,20,128]{2,1,0:T(8,128)} %gather_fusion), calls=%async_computation.1 | async-start | bytes 3145728 | tf_op jit(solution)/shard_map/all_to_all | solution.py:155
  262.9 2.5 sort.45
  267.5 2.5 sort.46
  270.7 30.7 %all-to-all-done = f32[128,20,128]{2,1,0:T(8,128)} async-done(((f32[128,20,128]{2,1,0:T(8,128)}), f32[128,20,128]{2,1,0:T(8,128)}, u32[]{:S(2)}, u32[]{:S(2)}) %all-to-all-start) | async-done | bytes 1310752 | tf_op jit(solution)/shard_map/all_to_all | solution.py:155
  301.4 2.1 gather_fusion.2
  303.4 66.9 %while.66 = (s32[]{:T(128)}, f32[128,20,128]{2,1,0:T(8,128)S(1)}, s32[]{:T(128)}, s32[128]{0:T(128)S(1)}, f32[128,20,20]{2,1,0:T(8,128)S(1)}, /*index=5*/f32[84,...) while((s32[]{:T(128)}, f32[128,20,128]{2,1,0:T(8,128)S(1)}, ...), condition=%wide.region_12.13_spmd, body=%wide.region_8.12_spmd.sunk | while | flops 370115008 | bytes 10114534 | solution.py:60
  305.6 12.1 %while.69 = (s32[]{:T(128)}, f32[128,20,128]{2,1,0:T(8,128)S(1)}, s32[]{:T(128)}, s32[128]{0:T(128)S(1)}, s32[]{:T(128)}, /*index=5*/f32[128,20,20]{2,1,0:T(8,12...) while((s32[]{:T(128)}, f32[128,20,128]{2,1,0:T(8,128)S(1)}, ...), condition=%wide.region_11.11_spmd, body=%wide.region_10.10_spmd.sunk | while | flops 370114624 | bytes 10113583 | solution.py:58
  305.6 2.4 fusion.83
  308.1 2.1 fusion.84
  311.7 2.4 fusion.83
  314.1 2.1 fusion.84
  319.7 12.0 %while.69 = (s32[]{:T(128)}, f32[128,20,128]{2,1,0:T(8,128)S(1)}, s32[]{:T(128)}, s32[128]{0:T(128)S(1)}, s32[]{:T(128)}, /*index=5*/f32[128,20,20]{2,1,0:T(8,12...) while((s32[]{:T(128)}, f32[128,20,128]{2,1,0:T(8,128)S(1)}, ...), condition=%wide.region_11.11_spmd, body=%wide.region_10.10_spmd.sunk | while | flops 370114624 | bytes 10113583 | solution.py:58
  319.7 2.4 fusion.83
  322.1 2.1 fusion.84
  325.7 2.4 fusion.83
  328.1 2.1 fusion.84
  333.7 12.0 %while.69 = (s32[]{:T(128)}, f32[128,20,128]{2,1,0:T(8,128)S(1)}, s32[]{:T(128)}, s32[128]{0:T(128)S(1)}, s32[]{:T(128)}, /*index=5*/f32[128,20,20]{2,1,0:T(8,12...) while((s32[]{:T(128)}, f32[128,20,128]{2,1,0:T(8,128)S(1)}, ...), condition=%wide.region_11.11_spmd, body=%wide.region_10.10_spmd.sunk | while | flops 370114624 | bytes 10113583 | solution.py:58
  333.7 2.4 fusion.83
  336.2 2.1 fusion.84
  339.7 2.4 fusion.83
  342.2 2.1 fusion.84
  347.7 6.0 %while.69 = (s32[]{:T(128)}, f32[128,20,128]{2,1,0:T(8,128)S(1)}, s32[]{:T(128)}, s32[128]{0:T(128)S(1)}, s32[]{:T(128)}, /*index=5*/f32[128,20,20]{2,1,0:T(8,12...) while((s32[]{:T(128)}, f32[128,20,128]{2,1,0:T(8,128)S(1)}, ...), condition=%wide.region_11.11_spmd, body=%wide.region_10.10_spmd.sunk | while | flops 370114624 | bytes 10113583 | solution.py:58
  347.8 2.4 fusion.83
  350.2 2.1 fusion.84
  355.8 6.0 %while.69 = (s32[]{:T(128)}, f32[128,20,128]{2,1,0:T(8,128)S(1)}, s32[]{:T(128)}, s32[128]{0:T(128)S(1)}, s32[]{:T(128)}, /*index=5*/f32[128,20,20]{2,1,0:T(8,12...) while((s32[]{:T(128)}, f32[128,20,128]{2,1,0:T(8,128)S(1)}, ...), condition=%wide.region_11.11_spmd, body=%wide.region_10.10_spmd.sunk | while | flops 370114624 | bytes 10113583 | solution.py:58
  355.8 2.4 fusion.83
  358.2 2.1 fusion.84
  363.8 6.0 %while.69 = (s32[]{:T(128)}, f32[128,20,128]{2,1,0:T(8,128)S(1)}, s32[]{:T(128)}, s32[128]{0:T(128)S(1)}, s32[]{:T(128)}, /*index=5*/f32[128,20,20]{2,1,0:T(8,12...) while((s32[]{:T(128)}, f32[128,20,128]{2,1,0:T(8,128)S(1)}, ...), condition=%wide.region_11.11_spmd, body=%wide.region_10.10_spmd.sunk | while | flops 370114624 | bytes 10113583 | solution.py:58
  363.8 2.4 fusion.83
  366.3 2.1 fusion.84
  370.4 1.9 gather_fusion.5
  372.3 2.7 all-to-all-start.2
  375.0 2.5 sort.47
  377.6 36.1 %all-to-all-done.2 = f32[128,20,128]{2,1,0:T(8,128)S(1)} async-done(((f32[128,20,128]{2,1,0:T(8,128)}), f32[128,20,128]{2,1,0:T(8,128)S(1)}, u32[]{:S(2)}, u32[]{:S(2)}) %all-to-all-start.2) | async-done | bytes 1310752 | tf_op jit(solution)/shard_map/all_to_all | solution.py:162
  (427 shorter events, 122.0 us)
Async XLA Ops:
  6.5 96.8 %copy-start = (s32[128]{0:T(128)S(1)}, s32[128]{0:T(128)}, u32[]{:S(2)}) copy-start(s32[128]{0:T(128)} %param.21) | copy-start | bytes 1540
  6.5 158.7 %reduce-scatter.2.cloned.1.call-start = ((), (), s32[]{:S(2)}) async-start(), calls=%async_computation.4 | async-start | bytes 110592 | tf_op jit(solution)/shard_map/reduce_scatter | solution.py:124
  6.5 3.6 copy-start.6
  10.6 1.1 copy-start.4
  13.4 2.4 copy-start.5
  15.8 1.1 copy-start.4
  18.6 2.4 copy-start.5
  21.0 1.1 copy-start.4
  23.8 2.4 copy-start.5
  26.3 1.1 copy-start.4
  29.1 2.4 copy-start.5
  31.5 1.1 copy-start.4
  34.3 2.4 copy-start.5
  36.7 1.1 copy-start.4
  39.5 2.4 copy-start.5
  42.0 1.1 copy-start.4
  44.8 2.4 copy-start.5
  47.2 1.1 copy-start.4
  50.0 2.4 copy-start.5
  52.5 1.1 copy-start.4
  55.2 2.4 copy-start.5
  57.7 1.1 copy-start.4
  60.5 2.4 copy-start.5
  62.9 1.1 copy-start.4
  65.7 2.4 copy-start.5
  68.2 1.1 copy-start.4
  71.0 2.4 copy-start.5
  73.4 1.1 copy-start.4
  76.2 2.4 copy-start.5
  78.6 1.1 copy-start.4
  81.4 2.4 copy-start.5
  83.9 1.1 copy-start.4
  86.7 2.4 copy-start.5
  89.1 1.1 copy-start.4
  91.9 2.4 copy-start.5
  94.4 9.0 %copy-start.9 = (s32[1,128]{1,0:T(1,128)S(1)}, s32[1,128]{1,0:T(1,128)}, u32[]{:S(2)}) copy-start(s32[1,128]{1,0:T(1,128)} %param.22) | copy-start | bytes 1540
  94.4 105.5 %copy-start.7 = (f32[128,128]{1,0:T(8,128)S(1)}, f32[128,128]{1,0:T(8,128)}, u32[]{:S(2)}) copy-start(f32[128,128]{1,0:T(8,128)} %param.19) | copy-start | bytes 196612
  94.7 3.7 collective-permute-start
  97.1 5.3 %collective-permute-start.1 = (f32[1,21,1024]{2,0,1:T(1,128)S(1)}, f32[1,21,1024]{2,0,1:T(1,128)S(1)}, u32[]{:S(2)}, u32[]{:S(2)}) collective-permute-start(f32[1,21,1024]{2,0,1:T(1,128)S(1)} %get-tuple-element.518), channel_id=1, source_target_pairs={{8,0},{16,8},{24,16},{9,1},{17,9},{25,17},{10,2},{18,10},{26,18},{... | collective-permute-start | bytes 258056 | tf_op jit(solution)/shard_map/ppermute | solution.py:20
  105.3 151.8 %all-to-all-start.1 = ((f32[32,4,1]{1,2,0:T(1,128)}), f32[32,4,1]{1,2,0:T(1,128)S(1)}, u32[]{:S(2)}, u32[]{:S(2)}) async-start(f32[32,4,1]{1,2,0:T(1,128)} %bitcast.18), calls=%async_computation.2 | async-start | bytes 32768 | tf_op jit(solution)/shard_map/all_to_all | solution.py:156
  197.2 2.6 collective-permute-start.2
  198.5 4.9 %collective-permute-start.3 = (f32[1,20,1024]{2,0,1:T(1,128)S(1)}, f32[1,20,1024]{2,0,1:T(1,128)S(1)}, u32[]{:S(2)}, u32[]{:S(2)}) collective-permute-start(f32[1,20,1024]{2,0,1:T(1,128)S(1)} %bitcast.108), channel_id=1, source_target_pairs={{8,0},{16,8},{24,16},{9,1},{17,9},{25,17},{10,2},{18,10},{26,18},{... | collective-permute-start | bytes 245768 | tf_op jit(solution)/shard_map/ppermute | solution.py:20
  253.0 1.3 copy-start.3
  257.1 5.5 %copy-start.8 = (f32[1,20,20]{2,0,1:T(1,128)S(1)}, f32[1,20,20]{2,0,1:T(1,128)}, u32[]{:S(2)}) copy-start(f32[1,20,20]{2,0,1:T(1,128)} %param.23) | copy-start | bytes 4804
  257.1 44.2 %all-to-all-start = ((f32[128,20,128]{2,1,0:T(8,128)}), f32[128,20,128]{2,1,0:T(8,128)}, u32[]{:S(2)}, u32[]{:S(2)}) async-start(f32[128,20,128]{2,1,0:T(8,128)} %gather_fusion), calls=%async_computation.1 | async-start | bytes 3145728 | tf_op jit(solution)/shard_map/all_to_all | solution.py:155
  270.6 32.8 %copy-start.1 = (f32[84,20]{0,1:T(8,128)S(1)}, f32[84,20]{0,1:T(8,128)}, u32[]{:S(2)}) copy-start(f32[84,20]{0,1:T(8,128)} %param.24) | copy-start | bytes 20164
  270.7 32.8 %copy-start.2 = (f32[20,84]{1,0:T(8,128)S(1)}, f32[20,84]{1,0:T(8,128)}, u32[]{:S(2)}) copy-start(f32[20,84]{1,0:T(8,128)} %param.25) | copy-start | bytes 20164
  372.3 41.4 %all-to-all-start.2 = ((f32[128,20,128]{2,1,0:T(8,128)}), f32[128,20,128]{2,1,0:T(8,128)S(1)}, u32[]{:S(2)}, u32[]{:S(2)}) async-start(f32[128,20,128]{2,1,0:T(8,128)} %gather_fusion.5), calls=%async_computation.3 | async-start | bytes 3145728 | tf_op jit(solution)/shard_map/all_to_all | solution.py:162
Sparse Core Ops, SparseCore 0:
  103.4 61.7 reduce-scatter.1
